TPU v7x, 128 devices: a whole 4x4x4 slice. The times are simulated.
128 devices in a mesh: grp: 8 (over x, y_hi), shard: 16 (over z, y_lo, core).
Axes of the slice: x: 4, y: 4 (y_hi: 2, y_lo: 2; y = y_hi * 2 + y_lo), z: 4, core: 2. Of those that a mesh axis runs over, the one named last changes fastest.
Arguments:
- points: bfloat16 [8, 24576, 1024], P('grp', 'shard'), may hold values from -6 to 6
- centroids: bfloat16 [8, 1024, 1024], P('grp', 'shard'), may hold values from -1.5 to 1.5
- tile_counts: int32 [8], replicated, may hold values from 97 to 192, as said below
Outputs:
- new_centroids: float32 [8, 1024, 1024], P('grp', 'shard')
- posterior_rows: bfloat16 [8, 24576, 1024], P('grp', 'shard')
Inputs may be any that keep to these rules, and one draw needn't show every extreme that they name: `tile_counts`: every coarse cluster has more than half of its 192 tile slots live, and some cluster has all 192.
All inputs are finite; a program needn't handle non-finite values.
Results may differ from a plain program's by a relative error of at most 0.0076.
Values may be sent and summed in bfloat16 or wider, within the bound.
A program may use at most 64 MiB of HBM per device.

v0:
```python
import jax
import jax.numpy as jnp
from jax import lax
from jax.sharding import PartitionSpec as P

TILE = 128
ITERS = 2
sharpness_factor = 48.0
epsilon = 1e-06


def partner(value, axis, bit):
    mask = 2**bit
    pairs = [(source, source ^ mask) for source in range(lax.axis_size(axis))]
    return lax.ppermute(value, axis, pairs)


def rms_unit(values):
    return values * lax.rsqrt(jnp.mean(values * values, axis=-1, keepdims=True) + epsilon)


def pick_entry(lookup_table, wanted):
    positions = jnp.arange(lookup_table.shape[0], dtype=jnp.int32)
    return jnp.sum(jnp.where(positions == wanted, lookup_table, 0))


def held_tiles(tile_total, shard_place, shard_count, slot_count):
    return jnp.clip((tile_total - shard_place + shard_count - 1) // shard_count, 0, slot_count)


def tile_weights(rows_per_tile, centroid_table):
    affinity_scores = lax.dot_general(
        rows_per_tile, centroid_table, (((1,), (1,)), ((), ())), preferred_element_type=jnp.float32
    ) * (sharpness_factor / rows_per_tile.shape[-1])
    exponent_terms = jnp.exp(affinity_scores)
    return (exponent_terms / jnp.sum(exponent_terms, axis=-1, keepdims=True)).astype(jnp.bfloat16)


def sweep(tile_stack, tile_limit, centroid_table, with_rows):
    centroid_count = centroid_table.shape[0]
    zero_sums = jnp.zeros((centroid_count, tile_stack.shape[2]), jnp.float32)
    zero_rows = jnp.zeros(tile_stack.shape, jnp.bfloat16)

    def visit(position, state_pair):
        running_sums, mean_rows = state_pair
        rows_per_tile = lax.dynamic_index_in_dim(tile_stack, position, 0, keepdims=False)
        weights = tile_weights(rows_per_tile, centroid_table)
        running_sums = running_sums + lax.dot_general(
            weights, rows_per_tile, (((0,), (0,)), ((), ())), preferred_element_type=jnp.float32
        )
        if with_rows:
            blended = jnp.dot(weights, centroid_table, preferred_element_type=jnp.float32).astype(
                jnp.bfloat16
            )
            mean_rows = lax.dynamic_update_index_in_dim(mean_rows, blended, position, 0)
        return (running_sums, mean_rows)

    return lax.fori_loop(0, tile_limit, visit, (zero_sums, zero_rows))


def body(points, centroids, tile_counts):
    slot_count = points.shape[1] // TILE
    half_slots = slot_count // 2
    feature_width = points.shape[2]
    shard_count = lax.axis_size("shard")
    shard_place = lax.axis_index("shard")
    group_index = lax.axis_index("grp")
    levels = lax.axis_size("grp").bit_length() - 1
    partner_bit = levels - 1
    unit_embeddings = rms_unit(points[0].astype(jnp.float32)).astype(jnp.bfloat16)
    tile_stack = unit_embeddings.reshape(slot_count, TILE, feature_width)
    own_held = held_tiles(
        pick_entry(tile_counts, group_index), shard_place, shard_count, slot_count
    )
    partner_group = jnp.bitwise_xor(group_index, 1 << partner_bit)
    partner_held = held_tiles(
        pick_entry(tile_counts, partner_group), shard_place, shard_count, slot_count
    )
    current_shard = centroids[0]
    borrowed = partner(tile_stack[half_slots:], "grp", partner_bit)
    updated = None
    out_rows = None
    for iteration in range(ITERS):
        is_last = iteration == ITERS - 1
        centroid_table = lax.all_gather(current_shard, "shard", axis=0, tiled=True)
        lent_piece = partner(current_shard, "grp", partner_bit)
        lent_table = lax.all_gather(lent_piece, "shard", axis=0, tiled=True)
        own_total, rows_low = sweep(
            tile_stack[:half_slots], jnp.minimum(own_held, half_slots), centroid_table, is_last
        )
        lent_limit = jnp.clip(partner_held - half_slots, 0, slot_count - half_slots)
        lent_total, rows_high = sweep(borrowed, lent_limit, lent_table, is_last)
        own_reduced, lent_reduced = (
            lax.psum_scatter(own_total, "shard", scatter_dimension=0, tiled=True),
            lax.psum_scatter(lent_total, "shard", scatter_dimension=0, tiled=True),
        )
        own_reduced = own_reduced + partner(lent_reduced, "grp", partner_bit)
        if is_last:
            returned_rows = partner(rows_high, "grp", partner_bit)
            out_rows = jnp.concatenate([rows_low, returned_rows], axis=0)
        updated = rms_unit(own_reduced)
        current_shard = updated.astype(jnp.bfloat16)
    return (updated[None], out_rows.reshape(1, slot_count * TILE, feature_width))


def solution(mesh):
    return jax.shard_map(
        body,
        mesh=mesh,
        in_specs=(P("grp", "shard", None), P("grp", "shard", None), P()),
        out_specs=(P("grp", "shard", None), P("grp", "shard", None)),
        check_vma=False,
    )
```

profile of v0, /device:TPU:6, one launch (start us, length us, event | category | flops | bytes accessed | tf_op | source)
XLA Modules:
  0.0 490.4 jit_solution(12478442984499041312)
XLA Ops:
  8.7 5.5 %collective-permute-done.1 = bf16[64,1024]{1,0:T(8,128)(2,1)S(1)} collective-permute-done((bf16[64,1024]{1,0:T(8,128)(2,1)}, bf16[64,1024]{1,0:T(8,128)(2,1)S(1)}, u32[]{:S(2)}, u32[]{:S(2)}) %collective-permute-start.1) | collective-permute-done | bytes 131104 | tf_op jit(solution)/shard_map/ppermute | solution.py:15
  15.0 2.6 fusion.34
  22.5 33.9 %collective-permute-done = bf16[6,128,1024]{2,1,0:T(8,128)(2,1)S(1)} collective-permute-done((bf16[6,128,1024]{2,1,0:T(8,128)(2,1)S(1)}, bf16[6,128,1024]{2,1,0:T(8,128)(2,1)S(1)}, u32[]{:S(2)}, u32[]{:S(2)}) %collective-permute-start) | collective-permute-done | bytes 1572896 | tf_op jit(solution)/shard_map/ppermute | solution.py:15
  57.6 2.5 broadcast.63.clone.2
  60.0 41.7 %while.45 = (s32[]{:T(128)}, f32[1024,1024]{1,0:T(8,128)}, s32[]{:T(128)}, bf16[6,128,1024]{2,1,0:T(8,128)(2,1)}, bf16[1024,1024]{1,0:T(8,128)(2,1)S(1)}, /*index=5*/s32[]{:T(128)}, s32[]{:T(128)}, s32[]{:T(128)}) while((s32[]{:T(128)}, f32[1024,1024]{1,0:T(8,128)}, s32[]{:T(128)}, bf16[6,128,1024]{2,1,0:T(8,128)(2,1)}, ...), condition=%wide.region_9.10_spmd, body=%wide.region_7.9_spmd.sunk | while | flops 538443648 | bytes 12059783 | solution.py:58
  60.0 1.9 fusion.70
  61.9 5.1 %convolution_add_fusion.9 = f32[1024,1024]{1,0:T(8,128)} fusion(f32[1024,1024]{1,0:T(8,128)} %get-tuple-element.381, f32[128,1024]{1,0:T(8,128)S(1)} %get-tuple-element.330, f32[128]{0:T(128)S(1)} %get-tuple-element.331, bf16[6,128,1024]{2,1,0:T(8,128)(2,1)} %get-tuple-element.391, s32[]{:T(128)S(6)} %select_n.46), kind=kOutput, calls=%fused_computation.11.clone.1 | convolution fusion | flops 269746176 | bytes 9175556 | tf_op jit(solution)/shard_map/while/body/dot_general | solution.py:48
  67.0 1.9 fusion.70
  68.8 5.1 %convolution_add_fusion.9 = f32[1024,1024]{1,0:T(8,128)} fusion(f32[1024,1024]{1,0:T(8,128)} %get-tuple-element.381, f32[128,1024]{1,0:T(8,128)S(1)} %get-tuple-element.330, f32[128]{0:T(128)S(1)} %get-tuple-element.331, bf16[6,128,1024]{2,1,0:T(8,128)(2,1)} %get-tuple-element.391, s32[]{:T(128)S(6)} %select_n.46), kind=kOutput, calls=%fused_computation.11.clone.1 | convolution fusion | flops 269746176 | bytes 9175556 | tf_op jit(solution)/shard_map/while/body/dot_general | solution.py:48
  74.0 1.9 fusion.70
  75.8 5.1 %convolution_add_fusion.9 = f32[1024,1024]{1,0:T(8,128)} fusion(f32[1024,1024]{1,0:T(8,128)} %get-tuple-element.381, f32[128,1024]{1,0:T(8,128)S(1)} %get-tuple-element.330, f32[128]{0:T(128)S(1)} %get-tuple-element.331, bf16[6,128,1024]{2,1,0:T(8,128)(2,1)} %get-tuple-element.391, s32[]{:T(128)S(6)} %select_n.46), kind=kOutput, calls=%fused_computation.11.clone.1 | convolution fusion | flops 269746176 | bytes 9175556 | tf_op jit(solution)/shard_map/while/body/dot_general | solution.py:48
  81.0 1.9 fusion.70
  82.8 5.1 %convolution_add_fusion.9 = f32[1024,1024]{1,0:T(8,128)} fusion(f32[1024,1024]{1,0:T(8,128)} %get-tuple-element.381, f32[128,1024]{1,0:T(8,128)S(1)} %get-tuple-element.330, f32[128]{0:T(128)S(1)} %get-tuple-element.331, bf16[6,128,1024]{2,1,0:T(8,128)(2,1)} %get-tuple-element.391, s32[]{:T(128)S(6)} %select_n.46), kind=kOutput, calls=%fused_computation.11.clone.1 | convolution fusion | flops 269746176 | bytes 9175556 | tf_op jit(solution)/shard_map/while/body/dot_general | solution.py:48
  87.9 1.9 fusion.70
  89.8 5.1 %convolution_add_fusion.9 = f32[1024,1024]{1,0:T(8,128)} fusion(f32[1024,1024]{1,0:T(8,128)} %get-tuple-element.381, f32[128,1024]{1,0:T(8,128)S(1)} %get-tuple-element.330, f32[128]{0:T(128)S(1)} %get-tuple-element.331, bf16[6,128,1024]{2,1,0:T(8,128)(2,1)} %get-tuple-element.391, s32[]{:T(128)S(6)} %select_n.46), kind=kOutput, calls=%fused_computation.11.clone.1 | convolution fusion | flops 269746176 | bytes 9175556 | tf_op jit(solution)/shard_map/while/body/dot_general | solution.py:48
  94.8 1.9 fusion.70
  96.7 5.1 %convolution_add_fusion.9 = f32[1024,1024]{1,0:T(8,128)} fusion(f32[1024,1024]{1,0:T(8,128)} %get-tuple-element.381, f32[128,1024]{1,0:T(8,128)S(1)} %get-tuple-element.330, f32[128]{0:T(128)S(1)} %get-tuple-element.331, bf16[6,128,1024]{2,1,0:T(8,128)(2,1)} %get-tuple-element.391, s32[]{:T(128)S(6)} %select_n.46), kind=kOutput, calls=%fused_computation.11.clone.1 | convolution fusion | flops 269746176 | bytes 9175556 | tf_op jit(solution)/shard_map/while/body/dot_general | solution.py:48
  102.5 2.5 broadcast.63.clone.1
  105.0 41.8 %while.44 = (s32[]{:T(128)}, f32[1024,1024]{1,0:T(8,128)}, s32[]{:T(128)}, bf16[6,128,1024]{2,1,0:T(8,128)(2,1)}, bf16[1024,1024]{1,0:T(8,128)(2,1)S(1)}, /*index=5*/s32[]{:T(128)}, s32[]{:T(128)}, s32[]{:T(128)}) while((s32[]{:T(128)}, f32[1024,1024]{1,0:T(8,128)}, s32[]{:T(128)}, bf16[6,128,1024]{2,1,0:T(8,128)(2,1)}, ...), condition=%wide.region_4.5_spmd, body=%wide.region_2.4_spmd.sunk | while | flops 538443648 | bytes 12059783 | solution.py:58
  105.0 1.9 fusion.67
  106.9 5.1 %convolution_add_fusion.8 = f32[1024,1024]{1,0:T(8,128)} fusion(f32[1024,1024]{1,0:T(8,128)} %get-tuple-element.357, f32[128,1024]{1,0:T(8,128)S(1)} %get-tuple-element.323, f32[128]{0:T(128)S(1)} %get-tuple-element.324, bf16[6,128,1024]{2,1,0:T(8,128)(2,1)} %get-tuple-element.367, s32[]{:T(128)S(6)} %select_n.45), kind=kOutput, calls=%fused_computation.clone.1 | convolution fusion | flops 269746176 | bytes 9175556 | tf_op jit(solution)/shard_map/while/body/dot_general | solution.py:48
  113.8 5.1 %convolution_add_fusion.8 = f32[1024,1024]{1,0:T(8,128)} fusion(f32[1024,1024]{1,0:T(8,128)} %get-tuple-element.357, f32[128,1024]{1,0:T(8,128)S(1)} %get-tuple-element.323, f32[128]{0:T(128)S(1)} %get-tuple-element.324, bf16[6,128,1024]{2,1,0:T(8,128)(2,1)} %get-tuple-element.367, s32[]{:T(128)S(6)} %select_n.45), kind=kOutput, calls=%fused_computation.clone.1 | convolution fusion | flops 269746176 | bytes 9175556 | tf_op jit(solution)/shard_map/while/body/dot_general | solution.py:48
  118.9 1.9 fusion.67
  120.7 5.1 %convolution_add_fusion.8 = f32[1024,1024]{1,0:T(8,128)} fusion(f32[1024,1024]{1,0:T(8,128)} %get-tuple-element.357, f32[128,1024]{1,0:T(8,128)S(1)} %get-tuple-element.323, f32[128]{0:T(128)S(1)} %get-tuple-element.324, bf16[6,128,1024]{2,1,0:T(8,128)(2,1)} %get-tuple-element.367, s32[]{:T(128)S(6)} %select_n.45), kind=kOutput, calls=%fused_computation.clone.1 | convolution fusion | flops 269746176 | bytes 9175556 | tf_op jit(solution)/shard_map/while/body/dot_general | solution.py:48
  125.8 1.9 fusion.67
  127.7 5.1 %convolution_add_fusion.8 = f32[1024,1024]{1,0:T(8,128)} fusion(f32[1024,1024]{1,0:T(8,128)} %get-tuple-element.357, f32[128,1024]{1,0:T(8,128)S(1)} %get-tuple-element.323, f32[128]{0:T(128)S(1)} %get-tuple-element.324, bf16[6,128,1024]{2,1,0:T(8,128)(2,1)} %get-tuple-element.367, s32[]{:T(128)S(6)} %select_n.45), kind=kOutput, calls=%fused_computation.clone.1 | convolution fusion | flops 269746176 | bytes 9175556 | tf_op jit(solution)/shard_map/while/body/dot_general | solution.py:48
  132.8 1.9 fusion.67
  134.7 5.1 %convolution_add_fusion.8 = f32[1024,1024]{1,0:T(8,128)} fusion(f32[1024,1024]{1,0:T(8,128)} %get-tuple-element.357, f32[128,1024]{1,0:T(8,128)S(1)} %get-tuple-element.323, f32[128]{0:T(128)S(1)} %get-tuple-element.324, bf16[6,128,1024]{2,1,0:T(8,128)(2,1)} %get-tuple-element.367, s32[]{:T(128)S(6)} %select_n.45), kind=kOutput, calls=%fused_computation.clone.1 | convolution fusion | flops 269746176 | bytes 9175556 | tf_op jit(solution)/shard_map/while/body/dot_general | solution.py:48
  139.8 1.9 fusion.67
  141.7 5.1 %convolution_add_fusion.8 = f32[1024,1024]{1,0:T(8,128)} fusion(f32[1024,1024]{1,0:T(8,128)} %get-tuple-element.357, f32[128,1024]{1,0:T(8,128)S(1)} %get-tuple-element.323, f32[128]{0:T(128)S(1)} %get-tuple-element.324, bf16[6,128,1024]{2,1,0:T(8,128)(2,1)} %get-tuple-element.367, s32[]{:T(128)S(6)} %select_n.45), kind=kOutput, calls=%fused_computation.clone.1 | convolution fusion | flops 269746176 | bytes 9175556 | tf_op jit(solution)/shard_map/while/body/dot_general | solution.py:48
  146.9 26.0 %reduce-scatter.7.cloned.1.call-done = f32[64,1024]{1,0:T(8,128)} async-done(((f32[1024,1024]{1,0:T(8,128)}), f32[64,1024]{1,0:T(8,128)}) %reduce-scatter.7.cloned.1.call-update) | async-done | bytes 262160 | tf_op jit(solution)/shard_map/reduce_scatter | solution.py:95
  174.5 70.2 %reduce-scatter.5.cloned.1.call-done = f32[64,1024]{1,0:T(8,128)} async-done(((f32[1024,1024]{1,0:T(8,128)}), f32[64,1024]{1,0:T(8,128)}) %reduce-scatter.5.cloned.1.call-update) | async-done | bytes 262160 | tf_op jit(solution)/shard_map/reduce_scatter | solution.py:94
  247.5 4.9 %collective-permute-done.3 = bf16[64,1024]{1,0:T(8,128)(2,1)S(1)} collective-permute-done((bf16[64,1024]{1,0:T(8,128)(2,1)S(1)}, bf16[64,1024]{1,0:T(8,128)(2,1)S(1)}, u32[]{:S(2)}, u32[]{:S(2)}) %collective-permute-start.3) | collective-permute-done | bytes 131104 | tf_op jit(solution)/shard_map/ppermute | solution.py:15
  253.7 32.2 %all-gather.10.cloned.1.call-done = bf16[1024,1024]{1,0:T(8,128)(2,1)} async-done(((bf16[64,1024]{1,0:T(8,128)(2,1)}), bf16[1024,1024]{1,0:T(8,128)(2,1)}) %all-gather.10.cloned.1.call-update) | async-done | bytes 2097168 | tf_op jit(solution)/shard_map/all_gather | solution.py:87
  285.9 2.5 broadcast.63.clone.3
  289.8 49.0 %while.47 = (s32[]{:T(128)}, f32[1024,1024]{1,0:T(8,128)}, bf16[6,128,1024]{2,1,0:T(8,128)(2,1)}, s32[]{:T(128)}, bf16[6,128,1024]{2,1,0:T(8,128)(2,1)}, /*index...) while((s32[]{:T(128)}, f32[1024,1024]{1,0:T(8,128)}, bf16[6,128,1024]{2,1,0:T(8,128)(2,1)}, ...), condition=%wide.region_18.19_spmd, body=%wide.region_16.18_spmd.sunk | while | flops 807272320 | bytes 14943891 | solution.py:58
  289.8 1.9 fusion.79
  291.7 5.1 %convolution_add_fusion.11 = f32[1024,1024]{1,0:T(8,128)} fusion(f32[1024,1024]{1,0:T(8,128)} %get-tuple-element.433, bf16[6,128,1024]{2,1,0:T(8,128)(2,1)} %get-tuple-element.445, s32[]{:T(128)S(6)} %select_n.48, f32[128,1024]{1,0:T(8,128)S(1)} %get-tuple-element.346, f32[128]{0:T(128)S(1)} %get-tuple-element.347), kind=kOutput, calls=%fused_computation.35.clone.1 | convolution fusion | flops 269746176 | bytes 9175556 | tf_op jit(solution)/shard_map/while/body/dot_general | solution.py:48
  299.9 5.1 %convolution_add_fusion.11 = f32[1024,1024]{1,0:T(8,128)} fusion(f32[1024,1024]{1,0:T(8,128)} %get-tuple-element.433, bf16[6,128,1024]{2,1,0:T(8,128)(2,1)} %get-tuple-element.445, s32[]{:T(128)S(6)} %select_n.48, f32[128,1024]{1,0:T(8,128)S(1)} %get-tuple-element.346, f32[128]{0:T(128)S(1)} %get-tuple-element.347), kind=kOutput, calls=%fused_computation.35.clone.1 | convolution fusion | flops 269746176 | bytes 9175556 | tf_op jit(solution)/shard_map/while/body/dot_general | solution.py:48
  306.2 1.9 fusion.79
  308.1 5.1 %convolution_add_fusion.11 = f32[1024,1024]{1,0:T(8,128)} fusion(f32[1024,1024]{1,0:T(8,128)} %get-tuple-element.433, bf16[6,128,1024]{2,1,0:T(8,128)(2,1)} %get-tuple-element.445, s32[]{:T(128)S(6)} %select_n.48, f32[128,1024]{1,0:T(8,128)S(1)} %get-tuple-element.346, f32[128]{0:T(128)S(1)} %get-tuple-element.347), kind=kOutput, calls=%fused_computation.35.clone.1 | convolution fusion | flops 269746176 | bytes 9175556 | tf_op jit(solution)/shard_map/while/body/dot_general | solution.py:48
  314.4 1.9 fusion.79
  316.3 5.1 %convolution_add_fusion.11 = f32[1024,1024]{1,0:T(8,128)} fusion(f32[1024,1024]{1,0:T(8,128)} %get-tuple-element.433, bf16[6,128,1024]{2,1,0:T(8,128)(2,1)} %get-tuple-element.445, s32[]{:T(128)S(6)} %select_n.48, f32[128,1024]{1,0:T(8,128)S(1)} %get-tuple-element.346, f32[128]{0:T(128)S(1)} %get-tuple-element.347), kind=kOutput, calls=%fused_computation.35.clone.1 | convolution fusion | flops 269746176 | bytes 9175556 | tf_op jit(solution)/shard_map/while/body/dot_general | solution.py:48
  324.4 5.1 %convolution_add_fusion.11 = f32[1024,1024]{1,0:T(8,128)} fusion(f32[1024,1024]{1,0:T(8,128)} %get-tuple-element.433, bf16[6,128,1024]{2,1,0:T(8,128)(2,1)} %get-tuple-element.445, s32[]{:T(128)S(6)} %select_n.48, f32[128,1024]{1,0:T(8,128)S(1)} %get-tuple-element.346, f32[128]{0:T(128)S(1)} %get-tuple-element.347), kind=kOutput, calls=%fused_computation.35.clone.1 | convolution fusion | flops 269746176 | bytes 9175556 | tf_op jit(solution)/shard_map/while/body/dot_general | solution.py:48
  330.7 1.9 fusion.79
  332.6 5.1 %convolution_add_fusion.11 = f32[1024,1024]{1,0:T(8,128)} fusion(f32[1024,1024]{1,0:T(8,128)} %get-tuple-element.433, bf16[6,128,1024]{2,1,0:T(8,128)(2,1)} %get-tuple-element.445, s32[]{:T(128)S(6)} %select_n.48, f32[128,1024]{1,0:T(8,128)S(1)} %get-tuple-element.346, f32[128]{0:T(128)S(1)} %get-tuple-element.347), kind=kOutput, calls=%fused_computation.35.clone.1 | convolution fusion | flops 269746176 | bytes 9175556 | tf_op jit(solution)/shard_map/while/body/dot_general | solution.py:48
  338.9 2.5 broadcast.63.clone
  342.8 49.3 %while.46 = (s32[]{:T(128)}, f32[1024,1024]{1,0:T(8,128)}, bf16[6,128,1024]{2,1,0:T(8,128)(2,1)}, s32[]{:T(128)}, bf16[6,128,1024]{2,1,0:T(8,128)(2,1)}, /*index...) while((s32[]{:T(128)}, f32[1024,1024]{1,0:T(8,128)}, bf16[6,128,1024]{2,1,0:T(8,128)(2,1)}, ...), condition=%wide.region_14.15_spmd, body=%wide.region_12.14_spmd.sunk | while | flops 807272320 | bytes 14943891 | solution.py:58
  342.8 1.9 fusion.74
  344.6 5.3 %convolution_add_fusion.10 = f32[1024,1024]{1,0:T(8,128)} fusion(f32[1024,1024]{1,0:T(8,128)} %get-tuple-element.406, bf16[6,128,1024]{2,1,0:T(8,128)(2,1)} %get-tuple-element.418, s32[]{:T(128)S(6)} %select_n.47, f32[128,1024]{1,0:T(8,128)S(1)} %get-tuple-element.338, f32[128]{0:T(128)S(1)} %get-tuple-element.339), kind=kOutput, calls=%fused_computation.22.clone.1 | convolution fusion | flops 269746176 | bytes 9175556 | tf_op jit(solution)/shard_map/while/body/dot_general | solution.py:48
  351.1 1.9 fusion.74
  353.0 5.1 %convolution_add_fusion.10 = f32[1024,1024]{1,0:T(8,128)} fusion(f32[1024,1024]{1,0:T(8,128)} %get-tuple-element.406, bf16[6,128,1024]{2,1,0:T(8,128)(2,1)} %get-tuple-element.418, s32[]{:T(128)S(6)} %select_n.47, f32[128,1024]{1,0:T(8,128)S(1)} %get-tuple-element.338, f32[128]{0:T(128)S(1)} %get-tuple-element.339), kind=kOutput, calls=%fused_computation.22.clone.1 | convolution fusion | flops 269746176 | bytes 9175556 | tf_op jit(solution)/shard_map/while/body/dot_general | solution.py:48
  359.3 1.9 fusion.74
  361.2 5.1 %convolution_add_fusion.10 = f32[1024,1024]{1,0:T(8,128)} fusion(f32[1024,1024]{1,0:T(8,128)} %get-tuple-element.406, bf16[6,128,1024]{2,1,0:T(8,128)(2,1)} %get-tuple-element.418, s32[]{:T(128)S(6)} %select_n.47, f32[128,1024]{1,0:T(8,128)S(1)} %get-tuple-element.338, f32[128]{0:T(128)S(1)} %get-tuple-element.339), kind=kOutput, calls=%fused_computation.22.clone.1 | convolution fusion | flops 269746176 | bytes 9175556 | tf_op jit(solution)/shard_map/while/body/dot_general | solution.py:48
  367.5 1.9 fusion.74
  369.4 5.1 %convolution_add_fusion.10 = f32[1024,1024]{1,0:T(8,128)} fusion(f32[1024,1024]{1,0:T(8,128)} %get-tuple-element.406, bf16[6,128,1024]{2,1,0:T(8,128)(2,1)} %get-tuple-element.418, s32[]{:T(128)S(6)} %select_n.47, f32[128,1024]{1,0:T(8,128)S(1)} %get-tuple-element.338, f32[128]{0:T(128)S(1)} %get-tuple-element.339), kind=kOutput, calls=%fused_computation.22.clone.1 | convolution fusion | flops 269746176 | bytes 9175556 | tf_op jit(solution)/shard_map/while/body/dot_general | solution.py:48
  375.7 1.9 fusion.74
  377.6 5.1 %convolution_add_fusion.10 = f32[1024,1024]{1,0:T(8,128)} fusion(f32[1024,1024]{1,0:T(8,128)} %get-tuple-element.406, bf16[6,128,1024]{2,1,0:T(8,128)(2,1)} %get-tuple-element.418, s32[]{:T(128)S(6)} %select_n.47, f32[128,1024]{1,0:T(8,128)S(1)} %get-tuple-element.338, f32[128]{0:T(128)S(1)} %get-tuple-element.339), kind=kOutput, calls=%fused_computation.22.clone.1 | convolution fusion | flops 269746176 | bytes 9175556 | tf_op jit(solution)/shard_map/while/body/dot_general | solution.py:48
  383.9 1.9 fusion.74
  385.7 5.1 %convolution_add_fusion.10 = f32[1024,1024]{1,0:T(8,128)} fusion(f32[1024,1024]{1,0:T(8,128)} %get-tuple-element.406, bf16[6,128,1024]{2,1,0:T(8,128)(2,1)} %get-tuple-element.418, s32[]{:T(128)S(6)} %select_n.47, f32[128,1024]{1,0:T(8,128)S(1)} %get-tuple-element.338, f32[128]{0:T(128)S(1)} %get-tuple-element.339), kind=kOutput, calls=%fused_computation.22.clone.1 | convolution fusion | flops 269746176 | bytes 9175556 | tf_op jit(solution)/shard_map/while/body/dot_general | solution.py:48
  393.5 14.8 %reduce-scatter.11.cloned.1.call-done = f32[64,1024]{1,0:T(8,128)} async-done(((f32[1024,1024]{1,0:T(8,128)}), f32[64,1024]{1,0:T(8,128)}) %reduce-scatter.11.cloned.1.call-update) | async-done | bytes 262160 | tf_op jit(solution)/shard_map/reduce_scatter | solution.py:95
  409.3 23.1 %collective-permute-done.5 = bf16[6,128,1024]{2,1,0:T(8,128)(2,1)} collective-permute-done((bf16[6,128,1024]{2,1,0:T(8,128)(2,1)S(1)}, bf16[6,128,1024]{2,1,0:T(8,128)(2,1)}, u32[]{:S(2)}, u32[]{:S(2)}) %collective-permute-start.5) | collective-permute-done | bytes 1572896 | tf_op jit(solution)/shard_map/ppermute | solution.py:15
  432.3 3.3 pad_maximum_fusion
  435.7 46.0 %reduce-scatter.9.cloned.1.call-done = f32[64,1024]{1,0:T(8,128)} async-done(((f32[1024,1024]{1,0:T(8,128)}), f32[64,1024]{1,0:T(8,128)}) %reduce-scatter.9.cloned.1.call-update) | async-done | bytes 262160 | tf_op jit(solution)/shard_map/reduce_scatter | solution.py:94
  (78 shorter events, 40.7 us)
Async XLA Ops:
  7.2 10.4 %copy-start.5 = (bf16[1,1536,1024]{2,1,0:T(8,128)(2,1)S(1)}, bf16[1,1536,1024]{2,1,0:T(8,128)(2,1)}, u32[]{:S(2)}) copy-start(bf16[1,1536,1024]{2,1,0:T(8,128)(2,1)} %param.11) | copy-start | bytes 9437188
  7.2 50.4 %all-gather.6.cloned.1.call-start = ((), (), s32[]{:S(2)}) async-start(), calls=%async_computation.5 | async-start | bytes 2228224 | tf_op jit(solution)/shard_map/all_gather | solution.py:87
  7.2 7.0 %collective-permute-start.1 = (bf16[64,1024]{1,0:T(8,128)(2,1)}, bf16[64,1024]{1,0:T(8,128)(2,1)S(1)}, u32[]{:S(2)}, u32[]{:S(2)}) collective-permute-start(bf16[64,1024]{1,0:T(8,128)(2,1)} %bitcast.89), channel_id=1, source_target_pairs={{0,64},{16,80},{32,96},{48,112},{64,0},{80,16},{96,32},{112,48},{1... | collective-permute-start | bytes 393224 | tf_op jit(solution)/shard_map/ppermute | solution.py:15
  14.2 0.7 copy-start.9
  14.9 87.5 %all-gather.12.cloned.1.call-start = ((), (), s32[]{:S(2)}) async-start(), calls=%async_computation.11 | async-start | bytes 2228224 | tf_op jit(solution)/shard_map/all_gather | solution.py:85
  18.2 3.0 copy-start.11
  19.6 36.8 %collective-permute-start = (bf16[6,128,1024]{2,1,0:T(8,128)(2,1)S(1)}, bf16[6,128,1024]{2,1,0:T(8,128)(2,1)S(1)}, u32[]{:S(2)}, u32[]{:S(2)}) collective-permute-start(bf16[6,128,1024]{2,1,0:T(8,128)(2,1)S(1)} %bitcast.88), channel_id=1, source_target_pairs={{0,64},{16,80},{32,96},{48,112},{64,0},{80,16},{96,32},{112,48},{1... | collective-permute-start | bytes 4718600 | tf_op jit(solution)/shard_map/ppermute | solution.py:15
  21.1 151.8 %reduce-scatter.7.cloned.1.call-start = ((), (), s32[]{:S(2)}) async-start(), calls=%async_computation.6 | async-start | bytes 4456448 | tf_op jit(solution)/shard_map/reduce_scatter | solution.py:95
  56.4 1.1 copy-start.4
  57.6 2.5 copy-start.2
  101.8 142.9 %reduce-scatter.5.cloned.1.call-start = ((), (), s32[]{:S(2)}) async-start(), calls=%async_computation.4 | async-start | bytes 4456448 | tf_op jit(solution)/shard_map/reduce_scatter | solution.py:94
  102.5 2.5 copy-start
  146.8 139.1 %all-gather.10.cloned.1.call-start = ((), (), s32[]{:S(2)}) async-start(), calls=%async_computation.9 | async-start | bytes 2228224 | tf_op jit(solution)/shard_map/all_gather | solution.py:87
  172.9 71.8 %collective-permute-start.2 = (f32[64,1024]{1,0:T(8,128)}, f32[64,1024]{1,0:T(8,128)S(1)}, u32[]{:S(2)}, u32[]{:S(2)}) collective-permute-start(f32[64,1024]{1,0:T(8,128)} %reduce-scatter.7.cloned.1.call-done), channel_id=1, source_target_pairs={{0,64},{16,80},{32,96},{48,112},{64,0},{80,16},{96,32},{112,48},{1... | collective-permute-start | bytes 786440 | tf_op jit(solution)/shard_map/ppermute | solution.py:15
  245.9 7.3 %copy-start.8 = (bf16[64,1024]{1,0:T(8,128)(2,1)}, bf16[64,1024]{1,0:T(8,128)(2,1)S(1)}, u32[]{:S(2)}) copy-start(bf16[64,1024]{1,0:T(8,128)(2,1)S(1)} %multiply_convert_fusion) | copy-start | bytes 393220
  245.9 6.6 %collective-permute-start.3 = (bf16[64,1024]{1,0:T(8,128)(2,1)S(1)}, bf16[64,1024]{1,0:T(8,128)(2,1)S(1)}, u32[]{:S(2)}, u32[]{:S(2)}) collective-permute-start(bf16[64,1024]{1,0:T(8,128)(2,1)S(1)} %multiply_convert_fusion), channel_id=1, source_target_pairs={{0,64},{16,80},{32,96},{48,112},{64,0},{80,16},{96,32},{112,48},{1... | collective-permute-start | bytes 393224 | tf_op jit(solution)/shard_map/ppermute | solution.py:15
  252.4 0.7 copy-start.10
  253.1 85.8 %all-gather.8.cloned.1.call-start = ((), (), s32[]{:S(2)}) async-start(), calls=%async_computation.7 | async-start | bytes 2228224 | tf_op jit(solution)/shard_map/all_gather | solution.py:85
  253.7 154.6 %reduce-scatter.11.cloned.1.call-start = ((), (), s32[]{:S(2)}) async-start(), calls=%async_computation.10 | async-start | bytes 4456448 | tf_op jit(solution)/shard_map/reduce_scatter | solution.py:95
  285.9 3.9 copy-start.3
  338.9 142.8 %reduce-scatter.9.cloned.1.call-start = ((), (), s32[]{:S(2)}) async-start(), calls=%async_computation.8 | async-start | bytes 4456448 | tf_op jit(solution)/shard_map/reduce_scatter | solution.py:94
  338.9 3.8 copy-start.1
  392.0 1.4 copy-start.7
  392.0 40.3 %copy-start.6 = (bf16[6,128,1024]{2,1,0:T(8,128)(2,1)S(1)}, bf16[6,128,1024]{2,1,0:T(8,128)(2,1)}, u32[]{:S(2)}) copy-start(bf16[6,128,1024]{2,1,0:T(8,128)(2,1)} %get-tuple-element.130) | copy-start | bytes 4718596
  393.5 38.9 %collective-permute-start.5 = (bf16[6,128,1024]{2,1,0:T(8,128)(2,1)S(1)}, bf16[6,128,1024]{2,1,0:T(8,128)(2,1)}, u32[]{:S(2)}, u32[]{:S(2)}) collective-permute-start(bf16[6,128,1024]{2,1,0:T(8,128)(2,1)S(1)} %copy-done.7), channel_id=1, source_target_pairs={{0,64},{16,80},{32,96},{48,112},{64,0},{80,16},{96,32},{112,48},{1... | collective-permute-start | bytes 4718600 | tf_op jit(solution)/shard_map/ppermute | solution.py:15
  408.2 73.4 %collective-permute-start.4 = (f32[64,1024]{1,0:T(8,128)}, f32[64,1024]{1,0:T(8,128)S(1)}, u32[]{:S(2)}, u32[]{:S(2)}) collective-permute-start(f32[64,1024]{1,0:T(8,128)} %reduce-scatter.11.cloned.1.call-done), channel_id=1, source_target_pairs={{0,64},{16,80},{32,96},{48,112},{64,0},{80,16},{96,32},{112,48},{1... | collective-permute-start | bytes 786440 | tf_op jit(solution)/shard_map/ppermute | solution.py:15
Sparse Core Ops, SparseCore 0:
  15.1 36.2 all-gather.5
  53.0 33.6 all-gather.11
  101.9 70.9 reduce-scatter.6
  175.1 69.4 reduce-scatter.4
  253.2 32.6 all-gather.9
  288.0 33.8 all-gather.7
  339.0 69.2 reduce-scatter.10
  410.6 70.9 reduce-scatter.8
where the time goes:
time: 492 us; the launch traced here: 490 us
  waiting for transfers between devices  257 us (52%)
  matrix products  182 us (37%)
  local copies, waits for them, and re-layouts  18.1 us (4%)
  between operations  15.6 us (3%)
  other arithmetic  10.2 us (2%)
  starting transfers between devices  7.51 us (2%)
    dot_general x24, matrix products, visit(): lax.dot_general(weights, rows_per_tile, (((0,), (0,)), ((), ())), preferr...  122 us
    reduce_scatter x2, waiting for transfers between devices, body(): lax.psum_scatter(own_total, 'shard', scatter_dimension=0, tiled=True)  116 us
    ppermute x6, waiting for transfers between devices, partner(): return lax.ppermute(value, axis, pairs)  67.5 us
    dot_general x24, matrix products, tile_weights(): lax.dot_general(rows_per_tile, centroid_table, (((1,), (1,)), ((), ())),...  45 us
    reduce_scatter x2, waiting for transfers between devices, body(): lax.psum_scatter(lent_total, 'shard', scatter_dimension=0, tiled=True)  40.7 us
    all_gather x2, waiting for transfers between devices, body(): lent_table = lax.all_gather(lent_piece, 'shard', axis=0, tiled=True)  32.2 us
    dot_general x12, matrix products, visit(): jnp.dot(weights, centroid_table, preferred_element_type=jnp.float32)  14.5 us
    another operation x6, local copies, waits for them, and re-layouts  12.7 us
  transfers between devices with their start and end apart: 14, of which 9 were waited for; matrix products, arithmetic and copies ran while one was open for 41% of the time, Pallas kernels for 0%

commit v1 on v0

--- a/solution.py
+++ b/solution.py
@@ -82,9 +82,14 @@
     out_rows = None
     for iteration in range(ITERS):
         is_last = iteration == ITERS - 1
-        centroid_table = lax.all_gather(current_shard, "shard", axis=0, tiled=True)
         lent_piece = partner(current_shard, "grp", partner_bit)
-        lent_table = lax.all_gather(lent_piece, "shard", axis=0, tiled=True)
+        centroid_table, lent_table = jnp.split(
+            lax.all_gather(
+                jnp.concatenate([current_shard, lent_piece], axis=1), "shard", axis=0, tiled=True
+            ),
+            [current_shard.shape[1]],
+            axis=1,
+        )
         own_total, rows_low = sweep(
             tile_stack[:half_slots], jnp.minimum(own_held, half_slots), centroid_table, is_last
         )

time: 492 us -> 500 us (1.016)
  local copies, waits for them, and re-layouts: 18.1 us -> 47.6 us
  matrix products: 182 us -> 153 us
  waiting for transfers between devices: 257 us -> 263 us
    ppermute x6, waiting for transfers between devices: 67.5 us -> 26.7 us  [partner(): return lax.ppermute(value, axis, pairs)]
    dot_general x24, matrix products: 122 us -> 83.2 us  [visit(): lax.dot_general(weights, rows_per_tile, (((0,), (0,)), ((), ())), preferr...]
    all_gather x4 -> x2, waiting for transfers between devices: 32.2 us -> 67.6 us  [body(): lax.all_gather(jnp.concatenate([current_shard, lent_piece], axis=1), 'sha...]
    while x0 -> x60, local copies, waits for them, and re-layouts: none -> 23.5 us
    dot_general x24, matrix products: 45 us -> 55.5 us  [tile_weights(): lax.dot_general(rows_per_tile, centroid_table, (((1,), (1,)), ((), ())),...]
    split x0 -> x2, local copies, waits for them, and re-layouts: none -> 7.96 us  [body(): jnp.split(lax.all_gather(jnp.concatenate([current_shard, lent_piece], axi...]
    reduce_scatter x2, waiting for transfers between devices: 40.7 us -> 46.7 us  [body(): lax.psum_scatter(lent_total, 'shard', scatter_dimension=0, tiled=True)]
    reduce_scatter x2, waiting for transfers between devices: 116 us -> 122 us  [body(): lax.psum_scatter(own_total, 'shard', scatter_dimension=0, tiled=True)]
  transfers between devices with their start and end apart: 14 -> 12, of which waited for: 9 -> 9; matrix products, arithmetic and copies ran while one was open for 41% -> 18% of each run, Pallas kernels for 0% -> 0%
where the time goes in v1:
time: 500 us; the launch traced here: 499 us
  waiting for transfers between devices  263 us (53%)
  matrix products  153 us (31%)
  local copies, waits for them, and re-layouts  47.6 us (10%)
  between operations  15.5 us (3%)
  other arithmetic  12.6 us (3%)
  starting transfers between devices  7.04 us (1%)
    reduce_scatter x2, waiting for transfers between devices, body(): lax.psum_scatter(own_total, 'shard', scatter_dimension=0, tiled=True)  122 us
    dot_general x24, matrix products, visit(): lax.dot_general(weights, rows_per_tile, (((0,), (0,)), ((), ())), preferr...  83.2 us
    all_gather x2, waiting for transfers between devices, body(): lax.all_gather(jnp.concatenate([current_shard, lent_piece], axis=1), 'sha...  67.6 us
    dot_general x24, matrix products, tile_weights(): lax.dot_general(rows_per_tile, centroid_table, (((1,), (1,)), ((), ())),...  55.5 us
    reduce_scatter x2, waiting for transfers between devices, body(): lax.psum_scatter(lent_total, 'shard', scatter_dimension=0, tiled=True)  46.7 us
    ppermute x6, waiting for transfers between devices, partner(): return lax.ppermute(value, axis, pairs)  26.7 us
    while x60, local copies, waits for them, and re-layouts  23.5 us
    dot_general x12, matrix products, visit(): jnp.dot(weights, centroid_table, preferred_element_type=jnp.float32)  14.5 us
  transfers between devices with their start and end apart: 12, of which 9 were waited for; matrix products, arithmetic and copies ran while one was open for 18% of the time, Pallas kernels for 0%

profile of v1, /device:TPU:6, one launch (start us, length us, event | category | flops | bytes accessed | tf_op | source)
XLA Modules:
  0.0 499.0 jit_solution(11388093899001290789)
XLA Ops:
  8.7 5.5 %collective-permute-done = bf16[64,1024]{1,0:T(8,128)(2,1)S(1)} collective-permute-done((bf16[64,1024]{1,0:T(8,128)(2,1)}, bf16[64,1024]{1,0:T(8,128)(2,1)S(1)}, u32[]{:S(2)}, u32[]{:S(2)}) %collective-permute-start) | collective-permute-done | bytes 131104 | tf_op jit(solution)/shard_map/ppermute | solution.py:15
  15.9 2.6 fusion.34
  19.1 2.0 fusion.44
  23.9 31.8 %all-gather.3.cloned.1.call-done = bf16[1024,2048]{1,0:T(8,128)(2,1)} async-done(((bf16[64,2048]{1,0:T(8,128)(2,1)}), bf16[1024,2048]{1,0:T(8,128)(2,1)}) %all-gather.3.cloned.1.call-update) | async-done | bytes 4194320 | tf_op jit(solution)/shard_map/all_gather | solution.py:87
  55.7 4.0 fusion.43
  59.7 2.5 broadcast.63.clone.2
  62.2 45.9 %while.45 = (s32[]{:T(128)}, f32[1024,1024]{1,0:T(8,128)}, s32[]{:T(128)}, bf16[6,128,1024]{2,1,0:T(8,128)(2,1)}, bf16[1024,1024]{1,0:T(8,128)(2,1)}, /*index=5*/s32[]{:T(128)}, s32[]{:T(128)}, s32[]{:T(128)}) while((s32[]{:T(128)}, f32[1024,1024]{1,0:T(8,128)}, s32[]{:T(128)}, bf16[6,128,1024]{2,1,0:T(8,128)(2,1)}, ...), condition=%wide.region_9.10_spmd, body=%wide.region_7.9_spmd.sunk | while | flops 538443648 | bytes 12059783 | solution.py:58
  62.2 2.6 fusion.72
  64.8 5.0 %convolution_add_fusion.9 = f32[1024,1024]{1,0:T(8,128)} fusion(f32[1024,1024]{1,0:T(8,128)} %get-tuple-element.385, f32[128,1024]{1,0:T(8,128)S(1)} %get-tuple-element.334, f32[128]{0:T(128)S(1)} %get-tuple-element.335, bf16[6,128,1024]{2,1,0:T(8,128)(2,1)} %get-tuple-element.395, s32[]{:T(128)S(6)} %select_n.46), kind=kOutput, calls=%fused_computation.11.clone.1 | convolution fusion | flops 269746176 | bytes 9175556 | tf_op jit(solution)/shard_map/while/body/dot_general | solution.py:48
  69.8 2.6 fusion.72
  72.4 5.0 %convolution_add_fusion.9 = f32[1024,1024]{1,0:T(8,128)} fusion(f32[1024,1024]{1,0:T(8,128)} %get-tuple-element.385, f32[128,1024]{1,0:T(8,128)S(1)} %get-tuple-element.334, f32[128]{0:T(128)S(1)} %get-tuple-element.335, bf16[6,128,1024]{2,1,0:T(8,128)(2,1)} %get-tuple-element.395, s32[]{:T(128)S(6)} %select_n.46), kind=kOutput, calls=%fused_computation.11.clone.1 | convolution fusion | flops 269746176 | bytes 9175556 | tf_op jit(solution)/shard_map/while/body/dot_general | solution.py:48
  77.5 2.6 fusion.72
  80.1 5.0 %convolution_add_fusion.9 = f32[1024,1024]{1,0:T(8,128)} fusion(f32[1024,1024]{1,0:T(8,128)} %get-tuple-element.385, f32[128,1024]{1,0:T(8,128)S(1)} %get-tuple-element.334, f32[128]{0:T(128)S(1)} %get-tuple-element.335, bf16[6,128,1024]{2,1,0:T(8,128)(2,1)} %get-tuple-element.395, s32[]{:T(128)S(6)} %select_n.46), kind=kOutput, calls=%fused_computation.11.clone.1 | convolution fusion | flops 269746176 | bytes 9175556 | tf_op jit(solution)/shard_map/while/body/dot_general | solution.py:48
  85.1 2.6 fusion.72
  87.7 5.0 %convolution_add_fusion.9 = f32[1024,1024]{1,0:T(8,128)} fusion(f32[1024,1024]{1,0:T(8,128)} %get-tuple-element.385, f32[128,1024]{1,0:T(8,128)S(1)} %get-tuple-element.334, f32[128]{0:T(128)S(1)} %get-tuple-element.335, bf16[6,128,1024]{2,1,0:T(8,128)(2,1)} %get-tuple-element.395, s32[]{:T(128)S(6)} %select_n.46), kind=kOutput, calls=%fused_computation.11.clone.1 | convolution fusion | flops 269746176 | bytes 9175556 | tf_op jit(solution)/shard_map/while/body/dot_general | solution.py:48
  92.8 2.6 fusion.72
  95.4 5.0 %convolution_add_fusion.9 = f32[1024,1024]{1,0:T(8,128)} fusion(f32[1024,1024]{1,0:T(8,128)} %get-tuple-element.385, f32[128,1024]{1,0:T(8,128)S(1)} %get-tuple-element.334, f32[128]{0:T(128)S(1)} %get-tuple-element.335, bf16[6,128,1024]{2,1,0:T(8,128)(2,1)} %get-tuple-element.395, s32[]{:T(128)S(6)} %select_n.46), kind=kOutput, calls=%fused_computation.11.clone.1 | convolution fusion | flops 269746176 | bytes 9175556 | tf_op jit(solution)/shard_map/while/body/dot_general | solution.py:48
  100.4 2.6 fusion.72
  103.0 5.0 %convolution_add_fusion.9 = f32[1024,1024]{1,0:T(8,128)} fusion(f32[1024,1024]{1,0:T(8,128)} %get-tuple-element.385, f32[128,1024]{1,0:T(8,128)S(1)} %get-tuple-element.334, f32[128]{0:T(128)S(1)} %get-tuple-element.335, bf16[6,128,1024]{2,1,0:T(8,128)(2,1)} %get-tuple-element.395, s32[]{:T(128)S(6)} %select_n.46), kind=kOutput, calls=%fused_computation.11.clone.1 | convolution fusion | flops 269746176 | bytes 9175556 | tf_op jit(solution)/shard_map/while/body/dot_general | solution.py:48
  108.8 2.5 broadcast.63.clone.1
  111.3 41.9 %while.44 = (s32[]{:T(128)}, f32[1024,1024]{1,0:T(8,128)}, s32[]{:T(128)}, bf16[6,128,1024]{2,1,0:T(8,128)(2,1)}, bf16[1024,1024]{1,0:T(8,128)(2,1)S(1)}, /*index=5*/s32[]{:T(128)}, s32[]{:T(128)}, s32[]{:T(128)}) while((s32[]{:T(128)}, f32[1024,1024]{1,0:T(8,128)}, s32[]{:T(128)}, bf16[6,128,1024]{2,1,0:T(8,128)(2,1)}, ...), condition=%wide.region_4.5_spmd, body=%wide.region_2.4_spmd.sunk | while | flops 538443648 | bytes 12059783 | solution.py:58
  113.1 5.1 %convolution_add_fusion.8 = f32[1024,1024]{1,0:T(8,128)} fusion(f32[1024,1024]{1,0:T(8,128)} %get-tuple-element.361, f32[128,1024]{1,0:T(8,128)S(1)} %get-tuple-element.327, f32[128]{0:T(128)S(1)} %get-tuple-element.328, bf16[6,128,1024]{2,1,0:T(8,128)(2,1)} %get-tuple-element.371, s32[]{:T(128)S(6)} %select_n.45), kind=kOutput, calls=%fused_computation.clone.1 | convolution fusion | flops 269746176 | bytes 9175556 | tf_op jit(solution)/shard_map/while/body/dot_general | solution.py:48
  120.1 5.1 %convolution_add_fusion.8 = f32[1024,1024]{1,0:T(8,128)} fusion(f32[1024,1024]{1,0:T(8,128)} %get-tuple-element.361, f32[128,1024]{1,0:T(8,128)S(1)} %get-tuple-element.327, f32[128]{0:T(128)S(1)} %get-tuple-element.328, bf16[6,128,1024]{2,1,0:T(8,128)(2,1)} %get-tuple-element.371, s32[]{:T(128)S(6)} %select_n.45), kind=kOutput, calls=%fused_computation.clone.1 | convolution fusion | flops 269746176 | bytes 9175556 | tf_op jit(solution)/shard_map/while/body/dot_general | solution.py:48
  127.1 5.1 %convolution_add_fusion.8 = f32[1024,1024]{1,0:T(8,128)} fusion(f32[1024,1024]{1,0:T(8,128)} %get-tuple-element.361, f32[128,1024]{1,0:T(8,128)S(1)} %get-tuple-element.327, f32[128]{0:T(128)S(1)} %get-tuple-element.328, bf16[6,128,1024]{2,1,0:T(8,128)(2,1)} %get-tuple-element.371, s32[]{:T(128)S(6)} %select_n.45), kind=kOutput, calls=%fused_computation.clone.1 | convolution fusion | flops 269746176 | bytes 9175556 | tf_op jit(solution)/shard_map/while/body/dot_general | solution.py:48
  134.0 5.1 %convolution_add_fusion.8 = f32[1024,1024]{1,0:T(8,128)} fusion(f32[1024,1024]{1,0:T(8,128)} %get-tuple-element.361, f32[128,1024]{1,0:T(8,128)S(1)} %get-tuple-element.327, f32[128]{0:T(128)S(1)} %get-tuple-element.328, bf16[6,128,1024]{2,1,0:T(8,128)(2,1)} %get-tuple-element.371, s32[]{:T(128)S(6)} %select_n.45), kind=kOutput, calls=%fused_computation.clone.1 | convolution fusion | flops 269746176 | bytes 9175556 | tf_op jit(solution)/shard_map/while/body/dot_general | solution.py:48
  141.0 5.1 %convolution_add_fusion.8 = f32[1024,1024]{1,0:T(8,128)} fusion(f32[1024,1024]{1,0:T(8,128)} %get-tuple-element.361, f32[128,1024]{1,0:T(8,128)S(1)} %get-tuple-element.327, f32[128]{0:T(128)S(1)} %get-tuple-element.328, bf16[6,128,1024]{2,1,0:T(8,128)(2,1)} %get-tuple-element.371, s32[]{:T(128)S(6)} %select_n.45), kind=kOutput, calls=%fused_computation.clone.1 | convolution fusion | flops 269746176 | bytes 9175556 | tf_op jit(solution)/shard_map/while/body/dot_general | solution.py:48
  148.0 5.1 %convolution_add_fusion.8 = f32[1024,1024]{1,0:T(8,128)} fusion(f32[1024,1024]{1,0:T(8,128)} %get-tuple-element.361, f32[128,1024]{1,0:T(8,128)S(1)} %get-tuple-element.327, f32[128]{0:T(128)S(1)} %get-tuple-element.328, bf16[6,128,1024]{2,1,0:T(8,128)(2,1)} %get-tuple-element.371, s32[]{:T(128)S(6)} %select_n.45), kind=kOutput, calls=%fused_computation.clone.1 | convolution fusion | flops 269746176 | bytes 9175556 | tf_op jit(solution)/shard_map/while/body/dot_general | solution.py:48
  153.2 24.8 %reduce-scatter.7.cloned.1.call-done = f32[64,1024]{1,0:T(8,128)} async-done(((f32[1024,1024]{1,0:T(8,128)}), f32[64,1024]{1,0:T(8,128)}) %reduce-scatter.7.cloned.1.call-update) | async-done | bytes 262160 | tf_op jit(solution)/shard_map/reduce_scatter | solution.py:100
  179.5 70.1 %reduce-scatter.5.cloned.1.call-done = f32[64,1024]{1,0:T(8,128)} async-done(((f32[1024,1024]{1,0:T(8,128)}), f32[64,1024]{1,0:T(8,128)}) %reduce-scatter.5.cloned.1.call-update) | async-done | bytes 262160 | tf_op jit(solution)/shard_map/reduce_scatter | solution.py:99
  252.5 4.9 collective-permute-done.3
  258.2 35.8 %all-gather.5.cloned.1.call-done = bf16[1024,2048]{1,0:T(8,128)(2,1)} async-done(((bf16[64,2048]{1,0:T(8,128)(2,1)}), bf16[1024,2048]{1,0:T(8,128)(2,1)}) %all-gather.5.cloned.1.call-update) | async-done | bytes 4194320 | tf_op jit(solution)/shard_map/all_gather | solution.py:87
  294.0 4.0 fusion.42
  299.4 2.5 broadcast.63.clone.3
  301.9 46.6 %while.47 = (s32[]{:T(128)}, f32[1024,1024]{1,0:T(8,128)}, bf16[6,128,1024]{2,1,0:T(8,128)(2,1)}, s32[]{:T(128)}, bf16[6,128,1024]{2,1,0:T(8,128)(2,1)}, /*index...) while((s32[]{:T(128)}, f32[1024,1024]{1,0:T(8,128)}, bf16[6,128,1024]{2,1,0:T(8,128)(2,1)}, ...), condition=%wide.region_18.19_spmd, body=%wide.region_16.18_spmd.sunk | while | flops 807272320 | bytes 56887012 | solution.py:58
  301.9 2.7 fusion.81
  307.7 1.9 copy-done.3
  309.7 2.7 fusion.81
  315.5 1.9 copy-done.3
  317.4 2.7 fusion.81
  323.3 1.9 copy-done.3
  325.2 2.7 fusion.81
  331.0 1.9 copy-done.3
  333.0 2.7 fusion.81
  338.8 1.9 copy-done.3
  340.7 2.7 fusion.81
  346.6 1.9 copy-done.3
  349.9 2.5 broadcast.63.clone
  352.4 42.6 %while.46 = (s32[]{:T(128)}, f32[1024,1024]{1,0:T(8,128)}, bf16[6,128,1024]{2,1,0:T(8,128)(2,1)}, s32[]{:T(128)}, bf16[6,128,1024]{2,1,0:T(8,128)(2,1)}, /*index...) while((s32[]{:T(128)}, f32[1024,1024]{1,0:T(8,128)}, bf16[6,128,1024]{2,1,0:T(8,128)(2,1)}, ...), condition=%wide.region_14.15_spmd, body=%wide.region_12.14_spmd.sunk | while | flops 807272320 | bytes 48498376 | solution.py:58
  352.4 2.0 fusion.76
  357.6 2.0 copy-done.1
  359.5 2.0 fusion.76
  364.7 2.0 copy-done.1
  366.6 2.0 fusion.76
  371.8 2.0 copy-done.1
  373.7 2.0 fusion.76
  378.9 2.0 copy-done.1
  380.8 2.0 fusion.76
  386.0 2.0 copy-done.1
  387.9 2.0 fusion.76
  393.1 2.0 copy-done.1
  396.5 21.9 %reduce-scatter.11.cloned.1.call-done = f32[64,1024]{1,0:T(8,128)} async-done(((f32[1024,1024]{1,0:T(8,128)}), f32[64,1024]{1,0:T(8,128)}) %reduce-scatter.11.cloned.1.call-update) | async-done | bytes 262160 | tf_op jit(solution)/shard_map/reduce_scatter | solution.py:100
  419.1 16.3 %collective-permute-done.5 = bf16[6,128,1024]{2,1,0:T(8,128)(2,1)} collective-permute-done((bf16[6,128,1024]{2,1,0:T(8,128)(2,1)S(1)}, bf16[6,128,1024]{2,1,0:T(8,128)(2,1)}, u32[]{:S(2)}, u32[]{:S(2)}) %collective-permute-start.5) | collective-permute-done | bytes 1572896 | tf_op jit(solution)/shard_map/ppermute | solution.py:15
  435.3 3.4 pad_maximum_fusion
  438.7 51.5 %reduce-scatter.9.cloned.1.call-done = f32[64,1024]{1,0:T(8,128)} async-done(((f32[1024,1024]{1,0:T(8,128)}), f32[64,1024]{1,0:T(8,128)}) %reduce-scatter.9.cloned.1.call-update) | async-done | bytes 262160 | tf_op jit(solution)/shard_map/reduce_scatter | solution.py:99
  (120 shorter events, 66.2 us)
Async XLA Ops:
  7.2 11.4 %copy-start.5 = (bf16[1,1536,1024]{2,1,0:T(8,128)(2,1)S(1)}, bf16[1,1536,1024]{2,1,0:T(8,128)(2,1)}, u32[]{:S(2)}) copy-start(bf16[1,1536,1024]{2,1,0:T(8,128)(2,1)} %param.11) | copy-start | bytes 9437188
  7.2 48.5 %all-gather.3.cloned.1.call-start = ((), (), s32[]{:S(2)}) async-start(), calls=%async_computation.4 | async-start | bytes 4456448 | tf_op jit(solution)/shard_map/all_gather | solution.py:87
  7.2 7.0 %collective-permute-start = (bf16[64,1024]{1,0:T(8,128)(2,1)}, bf16[64,1024]{1,0:T(8,128)(2,1)S(1)}, u32[]{:S(2)}, u32[]{:S(2)}) collective-permute-start(bf16[64,1024]{1,0:T(8,128)(2,1)} %bitcast.86), channel_id=1, source_target_pairs={{0,64},{16,80},{32,96},{48,112},{64,0},{80,16},{96,32},{112,48},{1... | collective-permute-start | bytes 393224 | tf_op jit(solution)/shard_map/ppermute | solution.py:15
  15.9 162.1 %reduce-scatter.7.cloned.1.call-start = ((), (), s32[]{:S(2)}) async-start(), calls=%async_computation.6 | async-start | bytes 4456448 | tf_op jit(solution)/shard_map/reduce_scatter | solution.py:100
  19.1 3.5 copy-start.8
  21.2 38.5 %collective-permute-start.1 = (bf16[6,128,1024]{2,1,0:T(8,128)(2,1)}, bf16[6,128,1024]{2,1,0:T(8,128)(2,1)}, u32[]{:S(2)}, u32[]{:S(2)}) collective-permute-start(bf16[6,128,1024]{2,1,0:T(8,128)(2,1)} %bitcast.10), channel_id=1, source_target_pairs={{0,64},{16,80},{32,96},{48,112},{64,0},{80,16},{96,32},{112,48},{1... | collective-permute-start | bytes 4718600 | tf_op jit(solution)/shard_map/ppermute | solution.py:15
  108.1 141.6 %reduce-scatter.5.cloned.1.call-start = ((), (), s32[]{:S(2)}) async-start(), calls=%async_computation.5 | async-start | bytes 4456448 | tf_op jit(solution)/shard_map/reduce_scatter | solution.py:99
  153.2 140.9 %all-gather.5.cloned.1.call-start = ((), (), s32[]{:S(2)}) async-start(), calls=%async_computation.7 | async-start | bytes 4456448 | tf_op jit(solution)/shard_map/all_gather | solution.py:87
  178.0 71.7 %collective-permute-start.2 = (f32[64,1024]{1,0:T(8,128)}, f32[64,1024]{1,0:T(8,128)S(1)}, u32[]{:S(2)}, u32[]{:S(2)}) collective-permute-start(f32[64,1024]{1,0:T(8,128)} %reduce-scatter.7.cloned.1.call-done), channel_id=1, source_target_pairs={{0,64},{16,80},{32,96},{48,112},{64,0},{80,16},{96,32},{112,48},{1... | collective-permute-start | bytes 786440 | tf_op jit(solution)/shard_map/ppermute | solution.py:15
  250.8 6.6 %collective-permute-start.3 = (bf16[64,1024]{1,0:T(8,128)(2,1)S(1)}, bf16[64,1024]{1,0:T(8,128)(2,1)S(1)}, u32[]{:S(2)}, u32[]{:S(2)}) collective-permute-start(bf16[64,1024]{1,0:T(8,128)(2,1)S(1)} %multiply_convert_fusion), channel_id=1, source_target_pairs={{0,64},{16,80},{32,96},{48,112},{64,0},{80,16},{96,32},{112,48},{1... | collective-permute-start | bytes 393224 | tf_op jit(solution)/shard_map/ppermute | solution.py:15
  258.1 160.2 %reduce-scatter.11.cloned.1.call-start = ((), (), s32[]{:S(2)}) async-start(), calls=%async_computation.9 | async-start | bytes 4456448 | tf_op jit(solution)/shard_map/reduce_scatter | solution.py:100
  301.9 2.7 copy-start.4
  301.9 4.0 copy-start.2
  307.7 1.9 copy-start.3
  309.7 2.7 copy-start.4
  309.7 4.0 copy-start.2
  315.5 1.9 copy-start.3
  317.4 2.7 copy-start.4
  317.4 3.9 copy-start.2
  323.2 1.9 copy-start.3
  325.2 2.7 copy-start.4
  325.2 4.0 copy-start.2
  331.0 1.9 copy-start.3
  333.0 2.7 copy-start.4
  333.0 4.0 copy-start.2
  338.8 1.9 copy-start.3
  340.7 2.7 copy-start.4
  340.7 4.0 copy-start.2
  346.6 1.9 copy-start.3
  348.5 141.7 %reduce-scatter.9.cloned.1.call-start = ((), (), s32[]{:S(2)}) async-start(), calls=%async_computation.8 | async-start | bytes 4456448 | tf_op jit(solution)/shard_map/reduce_scatter | solution.py:99
  352.4 3.2 copy-start
  357.6 2.0 copy-start.1
  359.5 3.2 copy-start
  364.7 2.0 copy-start.1
  366.6 3.2 copy-start
  371.7 2.0 copy-start.1
  373.7 3.2 copy-start
  378.8 2.0 copy-start.1
  380.8 3.2 copy-start
  385.9 2.0 copy-start.1
  387.9 3.2 copy-start
  393.0 2.0 copy-start.1
  395.0 1.4 copy-start.7
  395.0 40.3 %copy-start.6 = (bf16[6,128,1024]{2,1,0:T(8,128)(2,1)S(1)}, bf16[6,128,1024]{2,1,0:T(8,128)(2,1)}, u32[]{:S(2)}) copy-start(bf16[6,128,1024]{2,1,0:T(8,128)(2,1)} %get-tuple-element.130) | copy-start | bytes 4718596
  396.5 38.9 %collective-permute-start.5 = (bf16[6,128,1024]{2,1,0:T(8,128)(2,1)S(1)}, bf16[6,128,1024]{2,1,0:T(8,128)(2,1)}, u32[]{:S(2)}, u32[]{:S(2)}) collective-permute-start(bf16[6,128,1024]{2,1,0:T(8,128)(2,1)S(1)} %copy-done.7), channel_id=1, source_target_pairs={{0,64},{16,80},{32,96},{48,112},{64,0},{80,16},{96,32},{112,48},{1... | collective-permute-start | bytes 4718600 | tf_op jit(solution)/shard_map/ppermute | solution.py:15
  418.4 71.9 %collective-permute-start.4 = (f32[64,1024]{1,0:T(8,128)}, f32[64,1024]{1,0:T(8,128)S(1)}, u32[]{:S(2)}, u32[]{:S(2)}) collective-permute-start(f32[64,1024]{1,0:T(8,128)} %reduce-scatter.11.cloned.1.call-done), channel_id=1, source_target_pairs={{0,64},{16,80},{32,96},{48,112},{64,0},{80,16},{96,32},{112,48},{1... | collective-permute-start | bytes 786440 | tf_op jit(solution)/shard_map/ppermute | solution.py:15
Sparse Core Ops, SparseCore 0:
  16.0 39.6 all-gather.2
  108.2 69.7 reduce-scatter.6
  180.4 69.2 reduce-scatter.4
  258.3 35.7 all-gather.4
  348.7 69.6 reduce-scatter.10
  420.6 69.5 reduce-scatter.8
